TPU v7x, 32 devices: a whole 2x2x4 slice. The times are simulated.
32 devices in a mesh: batch: 4 (over z), seq: 2 (over core), ch: 4 (over y, x).
Axes of the slice: x: 2, y: 2, z: 4, core: 2. Of those that a mesh axis runs over, the one named last changes fastest.
Arguments:
- inputs: bfloat16 [16, 1280, 2048], P('batch', 'ch', 'seq'), may hold values from -6 to 6
- segment_ids: int32 [16, 2048], P('batch', 'seq'), may hold values from 0 to 7, never falling along the last dimension, each value on 1 to 512 neighbouring positions
- norm0_gain: float32 [1280], P('ch'), may hold values from 0.1 to 1.9
- norm0_shift: float32 [1280], P('ch'), may hold values from -3 to 3
- w_inner: bfloat16 [1280, 640], P('ch'), may hold values from -0.15625 to 0.15625
- b_inner: float32 [640], P('ch'), may hold values from -3 to 3
- norm1_gain: float32 [640], P('ch'), may hold values from 0.1 to 1.9
- norm1_shift: float32 [640], P('ch'), may hold values from -3 to 3
- w_conv: bfloat16 [5, 640, 640], P(None, 'ch'), may hold values from -0.109375 to 0.109375
- b_conv: float32 [640], P('ch'), may hold values from -3 to 3
- norm2_gain: float32 [640], P('ch'), may hold values from 0.1 to 1.9
- norm2_shift: float32 [640], P('ch'), may hold values from -3 to 3
- w_outer: bfloat16 [640, 1280], P('ch'), may hold values from -0.25 to 0.25
- b_outer: float32 [1280], P('ch'), may hold values from -3 to 3
- cotangent: bfloat16 [16, 1280, 2048], P('batch', 'ch', 'seq'), may hold values from -6 to 6
Outputs:
- output: bfloat16 [16, 1280, 2048], P('batch', 'ch', 'seq')
- input_grad: bfloat16 [16, 1280, 2048], P('batch', 'ch', 'seq')
- grad_norm0_gain: float32 [1280], P('ch')
- grad_norm0_shift: float32 [1280], P('ch')
- grad_w_inner: float32 [1280, 640], P('ch')
- grad_b_inner: float32 [640], P('ch')
- grad_norm1_gain: float32 [640], P('ch')
- grad_norm1_shift: float32 [640], P('ch')
- grad_w_conv: float32 [5, 640, 640], P(None, 'ch')
- grad_b_conv: float32 [640], P('ch')
- grad_norm2_gain: float32 [640], P('ch')
- grad_norm2_shift: float32 [640], P('ch')
- grad_w_outer: float32 [640, 1280], P('ch')
- grad_b_outer: float32 [1280], P('ch')
Inputs may be any that keep to these rules, and one draw needn't show every extreme that they name: `segment_ids`: along a row the ids never fall; each protein is one run of 1 to 512 residues, one run of each row has exactly 512, and every row holds all 8 ids.
All inputs are finite; a program needn't handle non-finite values.
Results may differ from a plain program's by a relative error of at most 0.0065.
Values may be sent and summed in bfloat16 or wider, within the bound.
A program may use at most 192 MiB of HBM per device.

v0:
```python
import jax
import jax.numpy as jnp
from jax import lax
from jax.sharding import PartitionSpec as P

KERNEL_TAPS = 5
DILATION_SPACING = 32
EPSILON = 1e-05


def gelu_exact(values):
    return jax.nn.gelu(values, approximate=False)


def gelu_back(point, grad):
    return jax.vjp(gelu_exact, point)[1](grad)[0]


def normalize(values, gain, shift):
    center = jnp.mean(values, axis=1, keepdims=True)
    offset = values - center
    spread = jnp.mean(offset * offset, axis=1, keepdims=True)
    scale = lax.rsqrt(spread + EPSILON)
    unit = offset * scale
    return (unit * gain[:, None] + shift[:, None], unit, scale)


def normalize_back(grad, unit, scale, gain):
    scaled = grad * gain[:, None]
    first = jnp.mean(scaled, axis=1, keepdims=True)
    second = jnp.mean(scaled * unit, axis=1, keepdims=True)
    return scale * (scaled - first - unit * second)


def neighbour_pairs(seqs, nch, q_count):
    pairs = []
    for s in range(seqs):
        for c in range(nch):
            q = c % q_count
            if q < q_count - 1:
                pairs.append((s * nch + c, s * nch + c + 1))
            elif s < seqs - 1:
                pairs.append((s * nch + c, (s + 1) * nch + c - (q_count - 1)))
    return pairs


def extended(x, width, pairs):
    down = [(j, i) for i, j in pairs]
    length = x.shape[-1]
    before = lax.ppermute(x[..., length - width :], ("seq", "ch"), pairs)
    after = lax.ppermute(x[..., :width], ("seq", "ch"), down)
    return jnp.concatenate([before, x, after], axis=-1)


def shifted_taps(wide, wide_ids, own_ids, offsets, border):
    length = own_ids.shape[-1]
    pieces = []
    for offset in offsets:
        lower = border + offset
        shifted = wide[:, :, lower : lower + length]
        matching = wide_ids[:, lower : lower + length] == own_ids
        pieces.append(jnp.where(matching[:, None, :], shifted, jnp.zeros_like(shifted)))
    return jnp.concatenate(pieces, axis=1)


def to_positions(x, nch, q_count):
    rows, width, length = x.shape
    if q_count > 1:
        x = x.reshape(rows, width, q_count, length // q_count).transpose(0, 2, 1, 3)
        x = x.reshape(rows * q_count, width, length // q_count)
    return lax.all_to_all(x, "ch", 0, 1, tiled=True)


def to_channels(x, nch, q_count, rows):
    x = lax.all_to_all(x, "ch", 1, 0, tiled=True)
    if q_count > 1:
        _, width, part = x.shape
        x = (
            x.reshape(rows, q_count, width, part)
            .transpose(0, 2, 1, 3)
            .reshape(rows, width, q_count * part)
        )
    return x


def local(
    inputs,
    segment_ids,
    norm0_gain,
    norm0_shift,
    w_inner,
    b_inner,
    norm1_gain,
    norm1_shift,
    w_conv,
    b_conv,
    norm2_gain,
    norm2_shift,
    w_outer,
    b_outer,
    cotangent,
):
    nch = lax.axis_size("ch")
    seqs = lax.axis_size("seq")
    batches = lax.axis_size("batch")
    rows, dloc, length = inputs.shape
    hloc = w_conv.shape[1]
    hid = hloc * nch
    dim = dloc * nch
    if rows % nch == 0:
        q_count = 1
    else:
        q_count = nch // rows
    part = length // q_count
    border = 2 * DILATION_SPACING
    offsets = [(k - KERNEL_TAPS // 2) * DILATION_SPACING for k in range(KERNEL_TAPS)]
    back_offsets = [-o for o in offsets]
    pairs = neighbour_pairs(seqs, nch, q_count)
    me = lax.axis_index("ch")
    smalls = [
        norm0_gain,
        norm0_shift,
        b_inner,
        norm1_gain,
        norm1_shift,
        b_conv,
        norm2_gain,
        norm2_shift,
        b_outer,
    ]
    small_all = lax.all_gather(jnp.concatenate(smalls), "ch", axis=0, tiled=False)
    cut = 0
    full = []
    for s in smalls:
        n = s.shape[0]
        full.append(small_all[:, cut : cut + n].reshape(n * nch))
        cut += n
    g0, s0, b_in, g1, s1, b_cv, g2, s2, b_out = full
    packed = jnp.concatenate([w_inner.reshape(-1), w_conv.reshape(-1), w_outer.reshape(-1)])
    packed_all = lax.all_gather(packed.reshape(1, -1, 128), "ch", axis=0, tiled=True).reshape(
        nch, -1
    )
    n_in, n_cv = (w_inner.size, w_conv.size)
    w_in = packed_all[:, :n_in].reshape(dim, hid)
    w_cv = (
        packed_all[:, n_in : n_in + n_cv]
        .reshape(nch, KERNEL_TAPS, hloc, hid)
        .transpose(1, 0, 2, 3)
        .reshape(KERNEL_TAPS, hid, hid)
    )
    w_out = packed_all[:, n_in + n_cv :].reshape(hid, dim)
    x = to_positions(inputs, nch, q_count)
    cot = to_positions(cotangent, nch, q_count)
    prow = x.shape[0]
    if q_count == 1:
        ids = lax.dynamic_slice_in_dim(segment_ids, me * prow, prow, axis=0)
    else:
        ids = lax.dynamic_slice_in_dim(segment_ids, me // q_count, 1, axis=0)
        ids = lax.dynamic_slice_in_dim(ids, me % q_count * part, part, axis=1)
    own_ids = ids + 1
    wide_ids = extended(own_ids, border, pairs)
    residual = x.astype(jnp.float32)
    normed0, unit0, scale0 = normalize(residual, g0, s0)
    hidden0 = gelu_exact(normed0).astype(jnp.bfloat16)
    inner = (
        jnp.einsum("dh,rdl->rhl", w_in, hidden0, preferred_element_type=jnp.float32) + b_in[:, None]
    )
    normed1, unit1, scale1 = normalize(inner, g1, s1)
    hidden1 = gelu_exact(normed1).astype(jnp.bfloat16)
    wide_hidden = extended(hidden1, border, pairs)
    taps = shifted_taps(wide_hidden, wide_ids, own_ids, offsets, border)
    kernel_flat = w_cv.reshape(KERNEL_TAPS * hid, hid)
    mixed = (
        jnp.einsum("co,rcl->rol", kernel_flat, taps, preferred_element_type=jnp.float32)
        + b_cv[:, None]
    )
    normed2, unit2, scale2 = normalize(mixed, g2, s2)
    hidden2 = gelu_exact(normed2).astype(jnp.bfloat16)
    branch = jnp.einsum("hd,rhl->rdl", w_out, hidden2, preferred_element_type=jnp.float32)
    output = (residual + branch + b_out[:, None]).astype(jnp.bfloat16)
    grad_b_outer = jnp.sum(cot.astype(jnp.float32), axis=(0, 2))
    grad_w_outer = jnp.einsum("rhl,rdl->hd", hidden2, cot, preferred_element_type=jnp.float32)
    grad_hidden2 = jnp.einsum("hd,rdl->rhl", w_out, cot, preferred_element_type=jnp.float32)
    grad_normed2 = gelu_back(normed2, grad_hidden2)
    grad_norm2_gain = jnp.sum(grad_normed2 * unit2, axis=(0, 2))
    grad_norm2_shift = jnp.sum(grad_normed2, axis=(0, 2))
    grad_mixed = normalize_back(grad_normed2, unit2, scale2, g2).astype(jnp.bfloat16)
    grad_b_conv = jnp.sum(grad_mixed.astype(jnp.float32), axis=(0, 2))
    grad_w_conv = jnp.einsum(
        "rcl,rol->co", taps, grad_mixed, preferred_element_type=jnp.float32
    ).reshape(KERNEL_TAPS, hid, hid)
    wide_grad = extended(grad_mixed, border, pairs)
    back_taps = shifted_taps(wide_grad, wide_ids, own_ids, back_offsets, border)
    kernel_back = jnp.transpose(w_cv, (0, 2, 1)).reshape(KERNEL_TAPS * hid, hid)
    grad_hidden1 = jnp.einsum(
        "oc,rol->rcl", kernel_back, back_taps, preferred_element_type=jnp.float32
    )
    grad_normed1 = gelu_back(normed1, grad_hidden1)
    grad_norm1_gain = jnp.sum(grad_normed1 * unit1, axis=(0, 2))
    grad_norm1_shift = jnp.sum(grad_normed1, axis=(0, 2))
    grad_inner = normalize_back(grad_normed1, unit1, scale1, g1).astype(jnp.bfloat16)
    grad_b_inner = jnp.sum(grad_inner.astype(jnp.float32), axis=(0, 2))
    grad_w_inner = jnp.einsum(
        "rdl,rhl->dh", hidden0, grad_inner, preferred_element_type=jnp.float32
    )
    grad_hidden0 = jnp.einsum("dh,rhl->rdl", w_in, grad_inner, preferred_element_type=jnp.float32)
    grad_normed0 = gelu_back(normed0, grad_hidden0)
    grad_norm0_gain = jnp.sum(grad_normed0 * unit0, axis=(0, 2))
    grad_norm0_shift = jnp.sum(grad_normed0, axis=(0, 2))
    input_grad = (cot.astype(jnp.float32) + normalize_back(grad_normed0, unit0, scale0, g0)).astype(
        jnp.bfloat16
    )
    output = to_channels(output, nch, q_count, rows)
    input_grad = to_channels(input_grad, nch, q_count, rows)
    grads = [
        grad_norm0_gain,
        grad_norm0_shift,
        grad_w_inner,
        grad_b_inner,
        grad_norm1_gain,
        grad_norm1_shift,
        grad_w_conv.transpose(1, 0, 2),
        grad_b_conv,
        grad_norm2_gain,
        grad_norm2_shift,
        grad_w_outer,
        grad_b_outer,
    ]
    flat = [g.reshape(nch, -1) for g in grads]
    sizes = [f.shape[1] for f in flat]
    stack = jnp.concatenate(flat, axis=1)
    total = stack.shape[1]
    lanes = 128
    spread = seqs * batches * 8 * lanes
    padded = -(-total // spread) * spread
    if padded != total:
        stack = jnp.pad(stack, ((0, 0), (0, padded - total)))
    stack = stack.reshape(nch, padded // lanes, lanes)
    stack = lax.psum_scatter(stack, "seq", scatter_dimension=1, tiled=True)
    stack = lax.psum_scatter(stack, "batch", scatter_dimension=1, tiled=True)
    stack = lax.psum_scatter(stack, "ch", scatter_dimension=0, tiled=True)
    stack = lax.all_gather(stack, ("seq", "batch"), axis=1, tiled=True).reshape(padded)[:total]
    shard_shapes = [
        norm0_gain.shape,
        norm0_shift.shape,
        w_inner.shape,
        b_inner.shape,
        norm1_gain.shape,
        norm1_shift.shape,
        (hloc, KERNEL_TAPS, hid),
        b_conv.shape,
        norm2_gain.shape,
        norm2_shift.shape,
        w_outer.shape,
        b_outer.shape,
    ]
    outs = []
    cut = 0
    for n, shape in zip(sizes, shard_shapes):
        outs.append(stack[cut : cut + n].reshape(shape))
        cut += n
    outs[6] = outs[6].transpose(1, 0, 2)
    return (output, input_grad, *outs)


def solution(mesh):
    return jax.shard_map(
        local,
        mesh=mesh,
        in_specs=(
            P("batch", "ch", "seq"),
            P("batch", "seq"),
            P("ch"),
            P("ch"),
            P("ch", None),
            P("ch"),
            P("ch"),
            P("ch"),
            P(None, "ch", None),
            P("ch"),
            P("ch"),
            P("ch"),
            P("ch", None),
            P("ch"),
            P("batch", "ch", "seq"),
        ),
        out_specs=(
            P("batch", "ch", "seq"),
            P("batch", "ch", "seq"),
            P("ch"),
            P("ch"),
            P("ch", None),
            P("ch"),
            P("ch"),
            P("ch"),
            P(None, "ch", None),
            P("ch"),
            P("ch"),
            P("ch"),
            P("ch", None),
            P("ch"),
        ),
        check_vma=False,
    )
```

profile of v0, /device:TPU:0, one launch (start us, length us, event | category | flops | bytes accessed | tf_op | source)
XLA Modules:
  0.0 816.1 jit_solution(5555885793643184578)
XLA Ops:
  13.4 5.3 all-to-all-start
  22.4 49.7 %all-gather.1 = f32[4,1,1920]{2,1,0:T(1,128)S(1)} all-gather(f32[1,1,1920]{2,1,0:T(1,128)S(1)} %reshape.1500), channel_id=2, replica_groups=mesh['batch'=4,'seq'=2,'ch'=4] {'ch'}, dimensions={0}, use_global_device_ids=true | all-gather | bytes 38400 | tf_op jit(solution)/shard_map/all_gather | solution.py:131
  73.7 4.8 all-to-all-start.2
  81.5 14.8 %fusion.6 = bf16[1,1280,1,1,1,1,1024]{6,1,5,4,3,2,0:T(8,128)(2,1)} fusion(f32[1,1280,1,1,1,1,1024]{6,1,5,4,3,2,0:T(8,128)S(1)} %bitcast.270, f32[1280]{0:T(1024)S(1)} %add.153, f32[1280]{0:T(1024)S(1)} %mul.431, f32[1024]{0:T(1024)S(1)} %add_rsqrt_fusion.2, f32[1024]{0:T(1024)S(1)} %broadcast_multiply_fusion.8), kind=kLoop, calls=%fused_computation.11 | loop fusion | flops 90439680 | bytes 7882752 | tf_op jit(solution)/shard_map/convert_element_type | solution.py:164
  96.3 48.7 %all-gather.5.cloned.1.call-done = bf16[4,7200,128]{2,1,0:T(8,128)(2,1)} async-done(((bf16[1,7200,128]{2,1,0:T(8,128)(2,1)}), bf16[4,7200,128]{2,1,0:T(8,128)(2,1)}) %all-gather.5.cloned.1.call-update) | async-done | bytes 7372816 | tf_op jit(solution)/shard_map/all_gather | solution.py:140
  145.0 26.1 %copy.86 = bf16[1,4,7200,128]{3,1,2,0:T(4,128)(2,1)S(1)} copy(bf16[1,4,7200,128]{3,2,1,0:T(8,128)(2,1)} %bitcast.283) | data formatting | bytes 14745600
  178.4 4.5 fusion.72
  183.5 7.3 multiply_convert_fusion.1
  196.5 5.9 copy.61
  202.4 3.6 slice.212
  208.9 4.1 reshape.1474
  214.3 7.9 copy.66
  226.6 8.0 constant_dynamic-update-slice_fusion
  237.5 9.6 %copy.69 = bf16[1,3200,1024]{2,1,0:T(8,128)(2,1)} copy(bf16[1,3200,1024]{1,2,0:T(8,128)(2,1)} %fusion.97) | data formatting | bytes 13107200 | tf_op jit(solution)/shard_map/concatenate | solution.py:63
  247.0 9.1 %fusion.74 = (f32[1024]{0:T(1024)S(1)}, f32[1024,640]{1,0:T(8,128)S(1)}) fusion(f32[640]{0:T(1024)S(1)} %add.163, bf16[3200,640]{1,0:T(8,128)(2,1)} %bitcast.279, bf16[1,3200,1024]{1,2,0:T(8,128)(2,1)} %fusion.97), kind=kOutput, calls=%fused_computation.146 | convolution fusion | flops 4195613696 | bytes 13277696 | tf_op jit(solution)/shard_map/co,rcl->rol/dot_general | solution.py:174
  256.7 11.8 %fusion.105 = f32[640,1280]{1,0:T(8,128)} fusion(bf16[1280,1024]{1,0:T(8,128)(2,1)} %bitcast.15, f32[640]{0:T(1024)S(1)} %add.167, f32[640]{0:T(1024)S(1)} %mul.451, f32[1024]{0:T(1024)S(1)} %add_rsqrt_fusion, f32[1024]{0:T(1024)S(1)} %broadcast_multiply_fusion.4, f32[640]{0:T(1024)S(1)} %add.163, f32[1024,640]{1,0:T(8,128)S(1)} %get-tuple-element.121), kind=kOutput, calls=%fused_computation.218 | convolution fusion | flops 1723596800 | bytes 8535552 | tf_op jit(solution)/shard_map/rhl,rdl->hd/dot_general | solution.py:182
  268.6 12.4 %fusion.50 = (f32[640]{0:T(1024)S(1)}, f32[1024]{0:T(1024)S(1)}, f32[1024]{0:T(1024)S(1)}, f32[640]{0:T(1024)S(1)}, f32[1,640,1024]{1,2,0:T(8,128)}) fusion(f32[1024]{0:T(1024)S(1)} %add_rsqrt_fusion, f32[1024]{0:T(1024)S(1)} %broadcast_multiply_fusion.4, f32[640]{0:T(1024)S(1)} %add.163, f32[1024,640]{1,0:T(8,128)S(1)} %get-tuple-element.121, ...), kind=kOutput, calls=%fused_computation.93 | convolution fusion | flops 1732113152 | bytes 9531904 | tf_op jit(solution)/shard_map/hd,rdl->rhl/dot_general | solution.py:183
  284.3 5.2 reshape.1491
  293.9 7.6 convolution_bitcast_fusion
  301.4 9.7 %copy.71 = f32[640,5,640]{2,1,0:T(8,128)} copy(f32[640,5,640]{2,0,1:T(8,128)S(1)} %convolution_bitcast_fusion) | data formatting | bytes 16384000 | tf_op jit(solution)/shard_map/transpose | solution.py:222
  311.2 12.0 %reshape.1487 = f32[4,512000]{1,0:T(4,128)} reshape(f32[640,5,640]{2,1,0:T(8,128)} %copy.71) | data formatting | bytes 16384000 | tf_op jit(solution)/shard_map/reshape | solution.py:229
  326.9 13.5 %fusion.56 = (f32[640]{0:T(1024)S(1)}, f32[1024]{0:T(1024)S(1)}, f32[1024]{0:T(1024)S(1)}, f32[640]{0:T(1024)S(1)}, f32[1,640,1024]{1,2,0:T(8,128)}) fusion(f32[1024]{0:T(1024)S(1)} %add_rsqrt_fusion.1, f32[1024]{0:T(1024)S(1)} %broadcast_multiply_fusion.5, f32[640]{0:T(1024)S(1)} %add.156, f32[1024,640]{1,0:T(8,128)S(1)} %copy-done.2, f32[640]{0:T(1024)S(1)} %mul.441, ...), kind=kOutput, calls=%fused_computation.104 | convolution fusion | flops 4248695808 | bytes 15921664 | tf_op jit(solution)/shard_map/oc,rol->rcl/dot_general | solution.py:195
  340.5 3.3 convert_reduce_fusion.2
  343.9 6.0 fusion.57
  349.9 3.5 reshape.1482
  353.4 19.2 %multiply_reduce_fusion = (f32[1280]{0:T(1024)S(1)}, f32[1024]{0:T(1024)S(1)}, f32[1024]{0:T(1024)S(1)}, f32[1280]{0:T(1024)S(1)}, f32[1,1280,1024]{1,2,0:T(8,128)}) fusion(f32[1,1280,1024]{1,2,0:T(8,128)} %copy.61, f32[1024]{0:T(1024)S(1)} %copy-done.15, f32[1024]{0:T(1024)S(1)} %copy-done.17, f32[1280]{0:T(1024)S(1)} %copy-done.13, ...), kind=kOutput, calls=%fused_computation.24 | convolution fusion | flops 1785196032 | bytes 13471744 | tf_op jit(solution)/shard_map/dh,rhl->rdl/dot_general | solution.py:206
  381.6 43.2 %dynamic-update-slice.6 = f32[4,923520]{1,0:T(4,128)} dynamic-update-slice(f32[4,923520]{1,0:T(4,128)} %dynamic-update-slice.5, f32[4,512000]{1,0:T(4,128)} %reshape.1487, s32[]{} %constant.29, s32[]{} %constant.35) | dynamic-update-slice | bytes 16384004
  429.4 17.2 %dynamic-update-slice.10 = f32[4,923520]{1,0:T(4,128)} dynamic-update-slice(f32[4,923520]{1,0:T(4,128)} %dynamic-update-slice.9, f32[4,204800]{1,0:T(4,128)S(1)} %copy-done.7, s32[]{} %constant.29, s32[]{} %constant.146) | dynamic-update-slice | bytes 6553604
  448.0 12.8 %pad_bitcast_fusion = f32[1,4,7232,128]{3,1,2,0:T(4,128)} fusion(f32[4,923520]{1,0:T(4,128)} %dynamic-update-slice.11), kind=kLoop, calls=%fused_computation.1 | loop fusion | bytes 29587456
  460.8 11.4 %copy.85 = f32[1,4,7232,128]{3,2,1,0:T(8,128)} copy(f32[1,4,7232,128]{3,1,2,0:T(4,128)} %pad_bitcast_fusion) | data formatting | bytes 29622272
  472.2 24.9 %reduce-scatter.6.cloned.1.call-done = f32[4,3616,128]{2,1,0:T(8,128)} async-done(((f32[4,7232,128]{2,1,0:T(8,128)}), f32[4,3616,128]{2,1,0:T(8,128)}) %reduce-scatter.6.cloned.1.call-update) | async-done | bytes 7405584 | tf_op jit(solution)/shard_map/reduce_scatter | solution.py:239
  497.2 132.5 %reduce-scatter.8.cloned.1.call-done = f32[4,904,128]{2,1,0:T(8,128)} async-done(((f32[4,3616,128]{2,1,0:T(8,128)}), f32[4,904,128]{2,1,0:T(8,128)}) %reduce-scatter.8.cloned.1.call-update) | async-done | bytes 1851408 | tf_op jit(solution)/shard_map/reduce_scatter | solution.py:240
  629.7 37.5 %reduce-scatter.10.cloned.1.call-done = f32[1,904,128]{2,1,0:T(8,128)} async-done(((f32[4,904,128]{2,1,0:T(8,128)}), f32[1,904,128]{2,1,0:T(8,128)}) %reduce-scatter.10.cloned.1.call-update) | async-done | bytes 462864
  667.3 11.7 %fusion.12 = bf16[1,1280,1024]{1,2,0:T(8,128)(2,1)} fusion(f32[1,1280,1024]{1,2,0:T(8,128)} %copy.61, bf16[640,1280]{1,0:T(8,128)(2,1)} %reshape.1474, f32[1280]{0:T(1024)S(1)} %add.171, f32[640]{0:T(1024)S(1)} %add.167, f32[640]{0:T(1024)S(1)} %mul.451, f32[1024]{0:T(1024)S(1)} %add_rsqrt_fusion, f32[1024]{0:T(1024)S(1)} %broadcast_multiply_fusion.4, ...), kind=kOutput, calls=%fused_computation.18 | convolution fusion | flops 1727528960 | bytes 12145152 | tf_op jit(solution)/shard_map/hd,rhl->rdl/dot_general | solution.py:179
  679.0 11.6 %copy.62 = bf16[1,1280,1024]{2,0,1:T(2,128)(2,1)} copy(bf16[1,1280,1024]{1,2,0:T(8,128)(2,1)} %fusion.12) | data formatting | bytes 5242880 | tf_op jit(solution)/shard_map/convert_element_type | solution.py:180
  691.1 15.6 %reduce.29 = bf16[1280,1024]{1,0:T(8,128)(2,1)S(1)} reduce(bf16[1280,1,1024]{2,1,0:T(2,128)(2,1)} %bitcast.274, bf16[]{:T(256)} %broadcast.2394), dimensions={1}, to_apply=%bitcast.237.reduce_sub_computation | reduce | bytes 5242882
  709.9 4.6 all-to-all-start.1
  714.4 4.9 copy.67
  719.4 6.4 add_convert_fusion
  725.8 8.3 %copy.68 = bf16[1,1280,1024]{2,0,1:T(2,128)(2,1)} copy(bf16[1,1280,1024]{1,2,0:T(8,128)(2,1)S(1)} %add_convert_fusion) | data formatting | bytes 5242880 | tf_op jit(solution)/shard_map/convert_element_type | solution.py:210
  734.0 15.6 %reduce.30 = bf16[1280,1024]{1,0:T(8,128)(2,1)S(1)} reduce(bf16[1280,1,1024]{2,1,0:T(2,128)(2,1)} %bitcast.275, bf16[]{:T(256)} %broadcast.2394), dimensions={1}, to_apply=%bitcast.239.reduce_sub_computation | reduce | bytes 5242882
  749.6 3.2 reshape.1511
  752.8 4.3 all-to-all-start.3
  757.1 5.5 reshape.1510
  762.7 5.0 copy.77
  767.7 19.7 %all-to-all-done.3 = bf16[4,2,163840]{2,1,0:T(2,128)(2,1)S(1)} async-done(((bf16[4,2,163840]{2,1,0:T(2,128)(2,1)}), bf16[4,2,163840]{2,1,0:T(2,128)(2,1)S(1)}, u32[]{:S(2)}, u32[]{:S(2)}) %all-to-all-start.3) | async-done | bytes 2621472 | tf_op jit(solution)/shard_map/all_to_all | solution.py:75
  787.3 3.8 reshape.1512
  791.2 5.0 copy.78
  (173 shorter events, 83.5 us)
Async XLA Ops:
  7.2 137.8 %all-gather.5.cloned.1.call-start = ((), (), s32[]{:S(2)}) async-start(), calls=%async_computation.7 | async-start | bytes 9216000 | tf_op jit(solution)/shard_map/all_gather | solution.py:140
  13.2 9.0 %copy-start.22 = (f32[320]{0:T(512)S(1)}, f32[320]{0:T(512)}, u32[]{:S(2)}) copy-start(f32[320]{0:T(512)} %param.17) | copy-start | bytes 3844
  13.3 9.0 %copy-start.23 = (f32[320]{0:T(512)S(1)}, f32[320]{0:T(512)}, u32[]{:S(2)}) copy-start(f32[320]{0:T(512)} %param.18) | copy-start | bytes 3844
  13.3 9.0 %copy-start.24 = (f32[320]{0:T(512)S(1)}, f32[320]{0:T(512)}, u32[]{:S(2)}) copy-start(f32[320]{0:T(512)} %param.28) | copy-start | bytes 3844
  13.3 9.0 %copy-start.25 = (f32[160]{0:T(256)S(1)}, f32[160]{0:T(256)}, u32[]{:S(2)}) copy-start(f32[160]{0:T(256)} %param.20) | copy-start | bytes 1924
  13.3 9.0 %copy-start.26 = (f32[160]{0:T(256)S(1)}, f32[160]{0:T(256)}, u32[]{:S(2)}) copy-start(f32[160]{0:T(256)} %param.21) | copy-start | bytes 1924
  13.3 9.0 %copy-start.27 = (f32[160]{0:T(256)S(1)}, f32[160]{0:T(256)}, u32[]{:S(2)}) copy-start(f32[160]{0:T(256)} %param.22) | copy-start | bytes 1924
  13.3 9.0 %copy-start.28 = (f32[160]{0:T(256)S(1)}, f32[160]{0:T(256)}, u32[]{:S(2)}) copy-start(f32[160]{0:T(256)} %param.24) | copy-start | bytes 1924
  13.3 9.0 %copy-start.29 = (f32[160]{0:T(256)S(1)}, f32[160]{0:T(256)}, u32[]{:S(2)}) copy-start(f32[160]{0:T(256)} %param.25) | copy-start | bytes 1924
  13.3 9.0 %copy-start.30 = (f32[160]{0:T(256)S(1)}, f32[160]{0:T(256)}, u32[]{:S(2)}) copy-start(f32[160]{0:T(256)} %param.26) | copy-start | bytes 1924
  13.4 60.4 %all-to-all-start = ((bf16[4,320,1024]{2,1,0:T(8,128)(2,1)}), bf16[4,320,1024]{2,1,0:T(8,128)(2,1)S(1)}, u32[]{:S(2)}, u32[]{:S(2)}) async-start(bf16[4,320,1024]{2,1,0:T(8,128)(2,1)} %param.15), calls=%async_computation | async-start | bytes 5242880 | tf_op jit(solution)/shard_map/all_to_all | solution.py:71
  19.5 54.1 %collective-permute-start = (s32[1,64]{1,0:T(1,128)S(1)}, s32[1,64]{1,0:T(1,128)S(1)}, u32[]{:S(2)}, u32[]{:S(2)}) collective-permute-start(s32[1,64]{1,0:T(1,128)S(1)} %get-tuple-element.116), channel_id=1, source_target_pairs={{0,4},{1,5},{2,6},{3,7},{8,12},{9,13},{10,14},{11,15},{16,20},{17,... | collective-permute-start | bytes 776 | tf_op jit(solution)/shard_map/ppermute | solution.py:50
  20.9 52.6 %collective-permute-start.2 = (s32[1,64]{1,0:T(1,128)S(1)}, s32[1,64]{1,0:T(1,128)S(1)}, u32[]{:S(2)}, u32[]{:S(2)}) collective-permute-start(s32[1,64]{1,0:T(1,128)S(1)} %get-tuple-element.117), channel_id=1, source_target_pairs={{4,0},{5,1},{6,2},{7,3},{12,8},{13,9},{14,10},{15,11},{20,16},{21,... | collective-permute-start | bytes 776 | tf_op jit(solution)/shard_map/ppermute | solution.py:51
  73.1 7.3 copy-start.12
  73.6 6.9 copy-start.18
  73.7 120.1 %all-to-all-start.2 = ((bf16[4,320,1024]{2,1,0:T(8,128)(2,1)}), bf16[4,320,1024]{2,1,0:T(8,128)(2,1)}, u32[]{:S(2)}, u32[]{:S(2)}) async-start(bf16[4,320,1024]{2,1,0:T(8,128)(2,1)} %param.29), calls=%async_computation.2 | async-start | bytes 5242880 | tf_op jit(solution)/shard_map/all_to_all | solution.py:71
  78.5 418.6 %reduce-scatter.6.cloned.1.call-start = ((), (), s32[]{:S(2)}) async-start(), calls=%async_computation.8 | async-start | bytes 22216704 | tf_op jit(solution)/shard_map/reduce_scatter | solution.py:239
  79.2 2.3 copy-start
  79.6 16.6 %copy-start.14 = (f32[1024]{0:T(1024)}, f32[1024]{0:T(1024)S(1)}, u32[]{:S(2)}) copy-start(f32[1024]{0:T(1024)S(1)} %broadcast_multiply_fusion.8) | copy-start | bytes 12292
  80.4 15.9 %copy-start.16 = (f32[1024]{0:T(1024)}, f32[1024]{0:T(1024)S(1)}, u32[]{:S(2)}) copy-start(f32[1024]{0:T(1024)S(1)} %add_rsqrt_fusion.2) | copy-start | bytes 12292
  171.0 3.0 copy-start.6
  182.9 43.6 %copy-start.1 = (f32[1024,640]{1,0:T(8,128)}, f32[1024,640]{1,0:T(8,128)S(1)}, u32[]{:S(2)}) copy-start(f32[1024,640]{1,0:T(8,128)S(1)} %get-tuple-element.119) | copy-start | bytes 7864324
  190.8 1.1 copy-start.4
  191.8 30.4 %collective-permute-start.1 = (bf16[1,640,64]{1,2,0:T(8,128)(2,1)S(1)}, bf16[1,640,64]{1,2,0:T(8,128)(2,1)S(1)}, u32[]{:S(2)}, u32[]{:S(2)}) collective-permute-start(bf16[1,640,64]{1,2,0:T(8,128)(2,1)S(1)} %get-tuple-element.106), channel_id=1, source_target_pairs={{0,4},{1,5},{2,6},{3,7},{8,12},{9,13},{10,14},{11,15},{16,20},{17,... | collective-permute-start | bytes 245768 | tf_op jit(solution)/shard_map/ppermute | solution.py:50
  213.1 21.5 %collective-permute-start.3 = (bf16[1,640,64]{1,2,0:T(8,128)(2,1)S(1)}, bf16[1,640,64]{1,2,0:T(8,128)(2,1)S(1)}, u32[]{:S(2)}, u32[]{:S(2)}) collective-permute-start(bf16[1,640,64]{1,2,0:T(8,128)(2,1)S(1)} %get-tuple-element.105), channel_id=1, source_target_pairs={{4,0},{5,1},{6,2},{7,3},{12,8},{13,9},{14,10},{15,11},{20,16},{21,... | collective-permute-start | bytes 245768 | tf_op jit(solution)/shard_map/ppermute | solution.py:51
  222.2 2.9 copy-start.5
  256.2 12.4 %copy-start.8 = (f32[1024,640]{1,0:T(8,128)}, f32[1024,640]{1,0:T(8,128)S(1)}, u32[]{:S(2)}) copy-start(f32[1024,640]{1,0:T(8,128)S(1)} %get-tuple-element.121) | copy-start | bytes 7864324
  256.7 11.8 %copy-start.11 = (bf16[640,1280]{1,0:T(8,128)(2,1)S(1)}, bf16[640,1280]{1,0:T(8,128)(2,1)}, u32[]{:S(2)}) copy-start(bf16[640,1280]{1,0:T(8,128)(2,1)} %reshape.1474) | copy-start | bytes 4915204
  289.5 34.6 %collective-permute-start.5 = (bf16[1,640,64]{1,2,0:T(8,128)(2,1)S(1)}, bf16[1,640,64]{1,2,0:T(8,128)(2,1)S(1)}, u32[]{:S(2)}, u32[]{:S(2)}) collective-permute-start(bf16[1,640,64]{1,2,0:T(8,128)(2,1)S(1)} %get-tuple-element.103), channel_id=1, source_target_pairs={{0,4},{1,5},{2,6},{3,7},{8,12},{9,13},{10,14},{11,15},{16,20},{17,... | collective-permute-start | bytes 245768 | tf_op jit(solution)/shard_map/ppermute | solution.py:50
  292.6 30.6 %collective-permute-start.4 = (bf16[1,640,64]{1,2,0:T(8,128)(2,1)S(1)}, bf16[1,640,64]{1,2,0:T(8,128)(2,1)S(1)}, u32[]{:S(2)}, u32[]{:S(2)}) collective-permute-start(bf16[1,640,64]{1,2,0:T(8,128)(2,1)S(1)} %get-tuple-element.104), channel_id=1, source_target_pairs={{4,0},{5,1},{6,2},{7,3},{12,8},{13,9},{14,10},{15,11},{20,16},{21,... | collective-permute-start | bytes 245768 | tf_op jit(solution)/shard_map/ppermute | solution.py:51
  323.9 2.2 copy-start.10
  324.1 2.8 copy-start.2
  326.9 13.6 %copy-start.3 = (f32[1024,640]{1,0:T(8,128)S(1)}, f32[1024,640]{1,0:T(8,128)}, u32[]{:S(2)}) copy-start(f32[1024,640]{1,0:T(8,128)} %copy-done.1) | copy-start | bytes 7864324
  349.9 3.5 copy-start.13
  349.9 3.5 copy-start.15
  349.9 3.5 copy-start.17
  349.9 3.5 copy-start.19
  381.6 47.8 %copy-start.7 = (f32[4,204800]{1,0:T(4,128)S(1)}, f32[4,204800]{1,0:T(4,128)}, u32[]{:S(2)}) copy-start(f32[4,204800]{1,0:T(4,128)} %reshape.1491) | copy-start | bytes 9830404
  429.4 17.3 %copy-start.21 = (f32[4,320]{1,0:T(4,128)S(1)}, f32[4,320]{1,0:T(4,128)}, u32[]{:S(2)}) copy-start(f32[4,320]{1,0:T(4,128)} %convert_reduce_fusion.3) | copy-start | bytes 15364
  472.1 157.5 %reduce-scatter.8.cloned.1.call-start = ((), (), s32[]{:S(2)}) async-start(), calls=%async_computation.9 | async-start | bytes 9256960 | tf_op jit(solution)/shard_map/reduce_scatter | solution.py:240
  497.1 170.1 %copy-start.20 = (f32[4,320]{1,0:T(4,128)S(1)}, f32[4,320]{1,0:T(4,128)}, u32[]{:S(2)}) copy-start(f32[4,320]{1,0:T(4,128)} %get-tuple-element.114) | copy-start | bytes 15364
  497.1 170.2 %copy-start.9 = (f32[1024,640]{1,0:T(8,128)S(1)}, f32[1024,640]{1,0:T(8,128)}, u32[]{:S(2)}) copy-start(f32[1024,640]{1,0:T(8,128)} %copy-done.8) | copy-start | bytes 7864324
  497.2 170.1 %reduce-scatter.10.cloned.1.call-start = ((), (), s32[]{:S(2)}) async-start(), calls=%async_computation.11 | async-start | bytes 2314240
  629.7 166.5 %all-gather.7.cloned.1.call-start = ((), (), s32[]{:S(2)}) async-start(), calls=%async_computation.10 | async-start | bytes 4165632 | tf_op jit(solution)/shard_map/all_gather | solution.py:242
  709.9 43.0 %all-to-all-start.1 = ((bf16[4,2,163840]{2,1,0:T(2,128)(2,1)}), bf16[4,2,163840]{2,1,0:T(2,128)(2,1)}, u32[]{:S(2)}, u32[]{:S(2)}) async-start(bf16[4,2,163840]{2,1,0:T(2,128)(2,1)} %reshape.1509), calls=%async_computation.1 | async-start | bytes 5242880 | tf_op jit(solution)/shard_map/all_to_all | solution.py:75
  752.8 34.5 %all-to-all-start.3 = ((bf16[4,2,163840]{2,1,0:T(2,128)(2,1)}), bf16[4,2,163840]{2,1,0:T(2,128)(2,1)S(1)}, u32[]{:S(2)}, u32[]{:S(2)}) async-start(bf16[4,2,163840]{2,1,0:T(2,128)(2,1)} %reshape.1511), calls=%async_computation.3 | async-start | bytes 5242880 | tf_op jit(solution)/shard_map/all_to_all | solution.py:75
Sparse Core Ops, SparseCore 0:
  13.4 131.5 all-gather.4
  472.3 24.8 reduce-scatter.5
  499.5 130.0 reduce-scatter.7
  632.5 34.6 reduce-scatter.9
  668.7 42.8 all-gather.6
where the time goes:
time: 824 us; the launch traced here: 816 us
  local copies, waits for them, and re-layouts  273 us (33%)
  waiting for transfers between devices  263 us (32%)
  matrix products  95.8 us (12%)
  other arithmetic  90.6 us (11%)
  blocking collectives  49.7 us (6%)
  starting transfers between devices  29.4 us (4%)
  between operations  14.6 us (2%)
    unnamed x88, local copies, waits for them, and re-layouts  160 us
    reduce_scatter x1, waiting for transfers between devices, local(): stack = lax.psum_scatter(stack, 'batch', scatter_dimension=1, tiled=True)  132 us
    all_gather x1, blocking collectives, local(): lax.all_gather(jnp.concatenate(smalls), 'ch', axis=0, tiled=False)  49.7 us
    all_gather x1, waiting for transfers between devices, local(): lax.all_gather(packed.reshape(1, -1, 128), 'ch', axis=0, tiled=True)  48.7 us
    unnamed x10, other arithmetic  46 us
    unnamed x6, waiting for transfers between devices  37.6 us
    reduce_scatter x1, waiting for transfers between devices, local(): stack = lax.psum_scatter(stack, 'seq', scatter_dimension=1, tiled=True)  24.9 us
    reshape x11, local copies, waits for them, and re-layouts, local(): flat = [g.reshape(nch, -1) for g in grads]  21.3 us
  transfers between devices with their start and end apart: 15, of which 5 were waited for; matrix products, arithmetic and copies ran while one was open for 28% of the time, Pallas kernels for 0%

commit v1 on v0

--- a/solution.py
+++ b/solution.py
@@ -6,6 +6,17 @@
 KERNEL_TAPS = 5
 DILATION_SPACING = 32
 EPSILON = 1e-05
+
+
+def split_up(shard, dim, size):
+    before, after = (shard.shape[:dim], shard.shape[dim + 1 :])
+    return jnp.moveaxis(shard.reshape(*before, size, -1, *after), dim, 0)
+
+
+def laid_out(blocks, dim):
+    blocks = jnp.moveaxis(blocks, 0, dim)
+    lengths = blocks.shape
+    return blocks.reshape(*lengths[:dim], lengths[dim] * lengths[dim + 1], *lengths[dim + 2 :])
 
 
 def gelu_exact(values):
@@ -72,7 +83,14 @@
 
 
 def to_channels(x, nch, q_count, rows):
-    x = lax.all_to_all(x, "ch", 1, 0, tiled=True)
+    size, index = (lax.axis_size("ch"), lax.axis_index("ch"))
+    parts = split_up(x, 1, size)
+    finished = [parts[index]]
+    for step in range(1, size):
+        sent = parts[index ^ step]
+        finished.append(lax.ppermute(sent, "ch", [(i_2, i_2 ^ step) for i_2 in range(size)]))
+    parts = jnp.stack(finished)[index ^ jnp.arange(size)]
+    x = laid_out(parts, 0)
     if q_count > 1:
         _, width, part = x.shape
         x = (

time: 824 us -> 780 us (0.947)
  local copies, waits for them, and re-layouts: 273 us -> 241 us
  other arithmetic: 90.6 us -> 61.7 us
  waiting for transfers between devices: 263 us -> 281 us
    ppermute x0 -> x6, waiting for transfers between devices: none -> 37.2 us  [to_channels(): lax.ppermute(sent, 'ch', [(i_2, i_2 ^ step) for i_2 in range(size)])]
    unnamed x10 -> x8, other arithmetic: 46 us -> 14.9 us
    unnamed x88 -> x85, local copies, waits for them, and re-layouts: 160 us -> 133 us
    all_to_all x2 -> x0, waiting for transfers between devices: 19.7 us -> none  [to_channels(): x = lax.all_to_all(x, 'ch', 1, 0, tiled=True)]
    all_to_all x2 -> x0, starting transfers between devices: 8.88 us -> none  [to_channels(): x = lax.all_to_all(x, 'ch', 1, 0, tiled=True)]
    convert_element_type x1, local copies, waits for them, and re-layouts: 11.6 us -> 3.02 us  [local(): output = (residual + branch + b_out[:, None]).astype(jnp.bfloat16)]
  transfers between devices with their start and end apart: 15 -> 19, of which waited for: 5 -> 8; matrix products, arithmetic and copies ran while one was open for 28% -> 22% of each run, Pallas kernels for 0% -> 0%
where the time goes in v1:
time: 780 us; the launch traced here: 772 us
  waiting for transfers between devices  281 us (36%)
  local copies, waits for them, and re-layouts  241 us (31%)
  matrix products  95.8 us (12%)
  other arithmetic  61.7 us (8%)
  blocking collectives  49.7 us (6%)
  starting transfers between devices  28.2 us (4%)
  between operations  14.9 us (2%)
    unnamed x85, local copies, waits for them, and re-layouts  133 us
    reduce_scatter x1, waiting for transfers between devices, local(): stack = lax.psum_scatter(stack, 'batch', scatter_dimension=1, tiled=True)  132 us
    all_gather x1, blocking collectives, local(): lax.all_gather(jnp.concatenate(smalls), 'ch', axis=0, tiled=False)  49.7 us
    all_gather x1, waiting for transfers between devices, local(): lax.all_gather(packed.reshape(1, -1, 128), 'ch', axis=0, tiled=True)  48.7 us
    unnamed x6, waiting for transfers between devices  37.6 us
    ppermute x6, waiting for transfers between devices, to_channels(): lax.ppermute(sent, 'ch', [(i_2, i_2 ^ step) for i_2 in range(size)])  37.2 us
    reduce_scatter x1, waiting for transfers between devices, local(): stack = lax.psum_scatter(stack, 'seq', scatter_dimension=1, tiled=True)  24.9 us
    reshape x11, local copies, waits for them, and re-layouts, local(): flat = [g.reshape(nch, -1) for g in grads]  21.3 us
  transfers between devices with their start and end apart: 19, of which 8 were waited for; matrix products, arithmetic and copies ran while one was open for 22% of the time, Pallas kernels for 0%

profile of v1, /device:TPU:0, one launch (start us, length us, event | category | flops | bytes accessed | tf_op | source)
XLA Modules:
  0.0 772.4 jit_solution(14650904212294518329)
XLA Ops:
  13.4 5.3 all-to-all-start
  22.4 49.7 %all-gather.1 = f32[4,1,1920]{2,1,0:T(1,128)S(1)} all-gather(f32[1,1,1920]{2,1,0:T(1,128)S(1)} %reshape.1540), channel_id=2, replica_groups=mesh['batch'=4,'seq'=2,'ch'=4] {'ch'}, dimensions={0}, use_global_device_ids=true | all-gather | bytes 38400 | tf_op jit(solution)/shard_map/all_gather | solution.py:149
  73.7 4.8 all-to-all-start.1
  81.5 14.8 %fusion.6 = bf16[1,1280,1,1,1,1,1024]{6,1,5,4,3,2,0:T(8,128)(2,1)} fusion(f32[1,1280,1,1,1,1,1024]{6,1,5,4,3,2,0:T(8,128)S(1)} %bitcast.302, f32[1280]{0:T(1024)S(1)} %add.178, f32[1280]{0:T(1024)S(1)} %mul.431, f32[1024]{0:T(1024)S(1)} %add_rsqrt_fusion.2, f32[1024]{0:T(1024)S(1)} %broadcast_multiply_fusion.8), kind=kLoop, calls=%fused_computation.13 | loop fusion | flops 90439680 | bytes 7882752 | tf_op jit(solution)/shard_map/convert_element_type | solution.py:182
  96.2 48.7 %all-gather.5.cloned.1.call-done = bf16[4,7200,128]{2,1,0:T(8,128)(2,1)} async-done(((bf16[1,7200,128]{2,1,0:T(8,128)(2,1)}), bf16[4,7200,128]{2,1,0:T(8,128)(2,1)}) %all-gather.5.cloned.1.call-update) | async-done | bytes 7372816 | tf_op jit(solution)/shard_map/all_gather | solution.py:158
  145.0 26.1 %copy.100 = bf16[1,4,7200,128]{3,1,2,0:T(4,128)(2,1)S(1)} copy(bf16[1,4,7200,128]{3,2,1,0:T(8,128)(2,1)} %bitcast.313) | data formatting | bytes 14745600
  171.1 3.0 copy-done.6
  178.4 4.5 fusion.72
  183.5 7.3 multiply_convert_fusion.1
  193.8 2.7 convert_reduce_fusion.3
  196.5 5.9 copy.71
  202.4 3.6 slice.216
  208.9 4.1 reshape.1490
  214.3 7.9 %copy.79 = bf16[5,640,640]{2,1,0:T(8,128)(2,1)} copy(bf16[5,640,640]{1,2,0:T(8,128)(2,1)} %bitcast.306) | data formatting | bytes 8192000 | tf_op jit(solution)/shard_map/transpose | solution.py:212
  222.2 2.9 fusion.90
  226.6 8.0 %constant_dynamic-update-slice_fusion = bf16[1,3200,1024]{1,2,0:T(8,128)(2,1)} fusion(bf16[1,3200,1024]{1,2,0:T(8,128)(2,1)} %fusion.99, f32[640]{0:T(1024)S(1)} %add.185, f32[640]{0:T(1024)S(1)} %mul.441, f32[1024]{0:T(1024)S(1)} %add_rsqrt_fusion.1, f32[1024]{0:T(1024)S(1)} %broadcast_multiply_fusion.5, f32[640]{0:T(1024)S(1)} %add.181, ...), kind=kLoop, calls=%fused_computation.200 | loop fusion | flops 45875200 | bytes 3948032
  237.5 9.6 %copy.85 = bf16[1,3200,1024]{2,1,0:T(8,128)(2,1)} copy(bf16[1,3200,1024]{1,2,0:T(8,128)(2,1)} %fusion.97) | data formatting | bytes 13107200 | tf_op jit(solution)/shard_map/concatenate | solution.py:74
  247.0 9.1 %fusion.74 = (f32[1024]{0:T(1024)S(1)}, f32[1024,640]{1,0:T(8,128)S(1)}) fusion(f32[640]{0:T(1024)S(1)} %add.188, bf16[3200,640]{1,0:T(8,128)(2,1)} %bitcast.307, bf16[1,3200,1024]{1,2,0:T(8,128)(2,1)} %fusion.97), kind=kOutput, calls=%fused_computation.150 | convolution fusion | flops 4195613696 | bytes 13277696 | tf_op jit(solution)/shard_map/co,rcl->rol/dot_general | solution.py:192
  256.7 11.8 %fusion.106 = f32[640,1280]{1,0:T(8,128)} fusion(bf16[1280,1024]{1,0:T(8,128)(2,1)} %bitcast.27, f32[640]{0:T(1024)S(1)} %add.192, f32[640]{0:T(1024)S(1)} %mul.451, f32[1024]{0:T(1024)S(1)} %add_rsqrt_fusion, f32[1024]{0:T(1024)S(1)} %broadcast_multiply_fusion.4, f32[640]{0:T(1024)S(1)} %add.188, f32[1024,640]{1,0:T(8,128)S(1)} %get-tuple-element.115), kind=kOutput, calls=%fused_computation.233 | convolution fusion | flops 1723596800 | bytes 8535552 | tf_op jit(solution)/shard_map/rhl,rdl->hd/dot_general | solution.py:200
  268.6 12.4 %fusion.50 = (f32[640]{0:T(1024)S(1)}, f32[1024]{0:T(1024)S(1)}, f32[1024]{0:T(1024)S(1)}, f32[640]{0:T(1024)S(1)}, f32[1,640,1024]{1,2,0:T(8,128)}) fusion(f32[1024]{0:T(1024)S(1)} %add_rsqrt_fusion, f32[1024]{0:T(1024)S(1)} %broadcast_multiply_fusion.4, f32[640]{0:T(1024)S(1)} %add.188, f32[1024,640]{1,0:T(8,128)S(1)} %get-tuple-element.115, ...), kind=kOutput, calls=%fused_computation.97 | convolution fusion | flops 1732113152 | bytes 9531904 | tf_op jit(solution)/shard_map/hd,rdl->rhl/dot_general | solution.py:201
  281.1 3.1 convert_reduce_fusion.1
  284.3 5.2 reshape.1509
  289.5 3.0 collective-permute-start.8
  293.9 7.6 convolution_bitcast_fusion
  301.5 9.7 %copy.87 = f32[640,5,640]{2,1,0:T(8,128)} copy(f32[640,5,640]{2,0,1:T(8,128)S(1)} %convolution_bitcast_fusion) | data formatting | bytes 16384000 | tf_op jit(solution)/shard_map/transpose | solution.py:240
  311.2 12.0 %reshape.1505 = f32[4,512000]{1,0:T(4,128)} reshape(f32[640,5,640]{2,1,0:T(8,128)} %copy.87) | data formatting | bytes 16384000 | tf_op jit(solution)/shard_map/reshape | solution.py:247
  326.9 13.5 %fusion.56 = (f32[640]{0:T(1024)S(1)}, f32[1024]{0:T(1024)S(1)}, f32[1024]{0:T(1024)S(1)}, f32[640]{0:T(1024)S(1)}, f32[1,640,1024]{1,2,0:T(8,128)}) fusion(f32[1024]{0:T(1024)S(1)} %add_rsqrt_fusion.1, f32[1024]{0:T(1024)S(1)} %broadcast_multiply_fusion.5, f32[640]{0:T(1024)S(1)} %add.181, f32[1024,640]{1,0:T(8,128)S(1)} %copy-done.2, f32[640]{0:T(1024)S(1)} %mul.441, ...), kind=kOutput, calls=%fused_computation.108 | convolution fusion | flops 4248695808 | bytes 15921664 | tf_op jit(solution)/shard_map/oc,rol->rcl/dot_general | solution.py:213
  340.5 3.3 convert_reduce_fusion.2
  343.9 6.0 fusion.57
  349.9 3.5 reshape.1500
  353.4 19.2 %multiply_reduce_fusion = (f32[1280]{0:T(1024)S(1)}, f32[1024]{0:T(1024)S(1)}, f32[1024]{0:T(1024)S(1)}, f32[1280]{0:T(1024)S(1)}, f32[1,1280,1024]{1,2,0:T(8,128)}) fusion(f32[1,1280,1024]{1,2,0:T(8,128)} %copy.71, f32[1024]{0:T(1024)S(1)} %copy-done.17, f32[1024]{0:T(1024)S(1)} %copy-done.19, f32[1280]{0:T(1024)S(1)} %copy-done.15, ...), kind=kOutput, calls=%fused_computation.26 | convolution fusion | flops 1785196032 | bytes 13471744 | tf_op jit(solution)/shard_map/dh,rhl->rdl/dot_general | solution.py:224
  381.6 43.2 %dynamic-update-slice.6 = f32[4,923520]{1,0:T(4,128)} dynamic-update-slice(f32[4,923520]{1,0:T(4,128)} %dynamic-update-slice.5, f32[4,512000]{1,0:T(4,128)} %reshape.1505, s32[]{} %constant.28, s32[]{} %constant.34) | dynamic-update-slice | bytes 16384004
  429.2 17.2 %dynamic-update-slice.10 = f32[4,923520]{1,0:T(4,128)} dynamic-update-slice(f32[4,923520]{1,0:T(4,128)} %dynamic-update-slice.9, f32[4,204800]{1,0:T(4,128)S(1)} %copy-done.8, s32[]{} %constant.28, s32[]{} %constant.38) | dynamic-update-slice | bytes 6553604
  447.9 12.8 %pad_bitcast_fusion = f32[1,4,7232,128]{3,1,2,0:T(4,128)} fusion(f32[4,923520]{1,0:T(4,128)} %dynamic-update-slice.11), kind=kLoop, calls=%fused_computation.3 | loop fusion | bytes 29587456
  460.6 11.4 %copy.99 = f32[1,4,7232,128]{3,2,1,0:T(8,128)} copy(f32[1,4,7232,128]{3,1,2,0:T(4,128)} %pad_bitcast_fusion) | data formatting | bytes 29622272
  472.0 24.9 %reduce-scatter.6.cloned.1.call-done = f32[4,3616,128]{2,1,0:T(8,128)} async-done(((f32[4,7232,128]{2,1,0:T(8,128)}), f32[4,3616,128]{2,1,0:T(8,128)}) %reduce-scatter.6.cloned.1.call-update) | async-done | bytes 7405584 | tf_op jit(solution)/shard_map/reduce_scatter | solution.py:257
  497.0 132.5 %reduce-scatter.8.cloned.1.call-done = f32[4,904,128]{2,1,0:T(8,128)} async-done(((f32[4,3616,128]{2,1,0:T(8,128)}), f32[4,904,128]{2,1,0:T(8,128)}) %reduce-scatter.8.cloned.1.call-update) | async-done | bytes 1851408 | tf_op jit(solution)/shard_map/reduce_scatter | solution.py:258
  629.6 37.5 %reduce-scatter.10.cloned.1.call-done = f32[1,904,128]{2,1,0:T(8,128)} async-done(((f32[4,904,128]{2,1,0:T(8,128)}), f32[1,904,128]{2,1,0:T(8,128)}) %reduce-scatter.10.cloned.1.call-update) | async-done | bytes 462864
  667.2 5.1 copy.80
  672.3 11.7 %fusion.12 = bf16[1,1280,1024]{1,2,0:T(8,128)(2,1)} fusion(f32[1,1280,1024]{1,2,0:T(8,128)} %copy.71, bf16[640,1280]{1,0:T(8,128)(2,1)} %reshape.1490, f32[1280]{0:T(1024)S(1)} %add.196, f32[640]{0:T(1024)S(1)} %add.192, f32[640]{0:T(1024)S(1)} %mul.451, f32[1024]{0:T(1024)S(1)} %add_rsqrt_fusion, f32[1024]{0:T(1024)S(1)} %broadcast_multiply_fusion.4, ...), kind=kOutput, calls=%fused_computation.20 | convolution fusion | flops 1727528960 | bytes 12145152 | tf_op jit(solution)/shard_map/hd,rhl->rdl/dot_general | solution.py:197
  684.0 3.0 copy.72
  691.9 5.1 add_convert_fusion
  696.9 2.6 copy.81
  699.5 3.2 constant_dynamic-slice_fusion
  708.6 12.7 %collective-permute-done.5 = bf16[1,320,1024]{2,1,0:T(8,128)(2,1)} collective-permute-done((bf16[1,320,1024]{2,1,0:T(8,128)(2,1)}, bf16[1,320,1024]{2,1,0:T(8,128)(2,1)}, u32[]{:S(2)}, u32[]{:S(2)}) %collective-permute-start.5) | collective-permute-done | bytes 655392 | tf_op jit(solution)/shard_map/ppermute | solution.py:91
  725.4 10.0 %collective-permute-done.11 = bf16[1,320,1024]{2,1,0:T(8,128)(2,1)} collective-permute-done((bf16[1,320,1024]{2,1,0:T(8,128)(2,1)}, bf16[1,320,1024]{2,1,0:T(8,128)(2,1)}, u32[]{:S(2)}, u32[]{:S(2)}) %collective-permute-start.11) | collective-permute-done | bytes 655392 | tf_op jit(solution)/shard_map/ppermute | solution.py:91
  735.4 12.8 %collective-permute-done.10 = bf16[1,320,1024]{2,1,0:T(8,128)(2,1)} collective-permute-done((bf16[1,320,1024]{2,1,0:T(8,128)(2,1)}, bf16[1,320,1024]{2,1,0:T(8,128)(2,1)}, u32[]{:S(2)}, u32[]{:S(2)}) %collective-permute-start.10) | collective-permute-done | bytes 655392 | tf_op jit(solution)/shard_map/ppermute | solution.py:91
  761.3 2.4 reshape.1512
  (184 shorter events, 81.3 us)
Async XLA Ops:
  7.2 137.8 %all-gather.5.cloned.1.call-start = ((), (), s32[]{:S(2)}) async-start(), calls=%async_computation.5 | async-start | bytes 9216000 | tf_op jit(solution)/shard_map/all_gather | solution.py:158
  13.2 9.0 %copy-start.24 = (f32[320]{0:T(512)S(1)}, f32[320]{0:T(512)}, u32[]{:S(2)}) copy-start(f32[320]{0:T(512)} %param.17) | copy-start | bytes 3844
  13.3 9.0 %copy-start.25 = (f32[320]{0:T(512)S(1)}, f32[320]{0:T(512)}, u32[]{:S(2)}) copy-start(f32[320]{0:T(512)} %param.18) | copy-start | bytes 3844
  13.3 9.0 %copy-start.26 = (f32[320]{0:T(512)S(1)}, f32[320]{0:T(512)}, u32[]{:S(2)}) copy-start(f32[320]{0:T(512)} %param.28) | copy-start | bytes 3844
  13.3 9.0 %copy-start.27 = (f32[160]{0:T(256)S(1)}, f32[160]{0:T(256)}, u32[]{:S(2)}) copy-start(f32[160]{0:T(256)} %param.20) | copy-start | bytes 1924
  13.3 9.0 %copy-start.28 = (f32[160]{0:T(256)S(1)}, f32[160]{0:T(256)}, u32[]{:S(2)}) copy-start(f32[160]{0:T(256)} %param.21) | copy-start | bytes 1924
  13.3 9.0 %copy-start.29 = (f32[160]{0:T(256)S(1)}, f32[160]{0:T(256)}, u32[]{:S(2)}) copy-start(f32[160]{0:T(256)} %param.22) | copy-start | bytes 1924
  13.3 9.0 %copy-start.30 = (f32[160]{0:T(256)S(1)}, f32[160]{0:T(256)}, u32[]{:S(2)}) copy-start(f32[160]{0:T(256)} %param.24) | copy-start | bytes 1924
  13.3 9.0 %copy-start.31 = (f32[160]{0:T(256)S(1)}, f32[160]{0:T(256)}, u32[]{:S(2)}) copy-start(f32[160]{0:T(256)} %param.25) | copy-start | bytes 1924
  13.3 9.0 %copy-start.32 = (f32[160]{0:T(256)S(1)}, f32[160]{0:T(256)}, u32[]{:S(2)}) copy-start(f32[160]{0:T(256)} %param.26) | copy-start | bytes 1924
  13.4 60.4 %all-to-all-start = ((bf16[4,320,1024]{2,1,0:T(8,128)(2,1)}), bf16[4,320,1024]{2,1,0:T(8,128)(2,1)S(1)}, u32[]{:S(2)}, u32[]{:S(2)}) async-start(bf16[4,320,1024]{2,1,0:T(8,128)(2,1)} %param.15), calls=%async_computation | async-start | bytes 5242880 | tf_op jit(solution)/shard_map/all_to_all | solution.py:82
  19.5 54.1 %collective-permute-start = (s32[1,64]{1,0:T(1,128)S(1)}, s32[1,64]{1,0:T(1,128)S(1)}, u32[]{:S(2)}, u32[]{:S(2)}) collective-permute-start(s32[1,64]{1,0:T(1,128)S(1)} %get-tuple-element.110), channel_id=1, source_target_pairs={{0,4},{1,5},{2,6},{3,7},{8,12},{9,13},{10,14},{11,15},{16,20},{17,... | collective-permute-start | bytes 776 | tf_op jit(solution)/shard_map/ppermute | solution.py:61
  20.9 52.6 %collective-permute-start.2 = (s32[1,64]{1,0:T(1,128)S(1)}, s32[1,64]{1,0:T(1,128)S(1)}, u32[]{:S(2)}, u32[]{:S(2)}) collective-permute-start(s32[1,64]{1,0:T(1,128)S(1)} %get-tuple-element.111), channel_id=1, source_target_pairs={{4,0},{5,1},{6,2},{7,3},{12,8},{13,9},{14,10},{15,11},{20,16},{21,... | collective-permute-start | bytes 776 | tf_op jit(solution)/shard_map/ppermute | solution.py:62
  73.1 7.3 copy-start.14
  73.6 6.9 copy-start.20
  73.7 120.1 %all-to-all-start.1 = ((bf16[4,320,1024]{2,1,0:T(8,128)(2,1)}), bf16[4,320,1024]{2,1,0:T(8,128)(2,1)}, u32[]{:S(2)}, u32[]{:S(2)}) async-start(bf16[4,320,1024]{2,1,0:T(8,128)(2,1)} %param.29), calls=%async_computation.1 | async-start | bytes 5242880 | tf_op jit(solution)/shard_map/all_to_all | solution.py:82
  78.5 418.5 %reduce-scatter.6.cloned.1.call-start = ((), (), s32[]{:S(2)}) async-start(), calls=%async_computation.6 | async-start | bytes 22216704 | tf_op jit(solution)/shard_map/reduce_scatter | solution.py:257
  79.6 16.6 %copy-start.16 = (f32[1024]{0:T(1024)}, f32[1024]{0:T(1024)S(1)}, u32[]{:S(2)}) copy-start(f32[1024]{0:T(1024)S(1)} %broadcast_multiply_fusion.8) | copy-start | bytes 12292
  80.4 15.8 %copy-start.18 = (f32[1024]{0:T(1024)}, f32[1024]{0:T(1024)S(1)}, u32[]{:S(2)}) copy-start(f32[1024]{0:T(1024)S(1)} %add_rsqrt_fusion.2) | copy-start | bytes 12292
  171.0 3.0 copy-start.6
  182.9 43.7 %copy-start.1 = (f32[1024,640]{1,0:T(8,128)}, f32[1024,640]{1,0:T(8,128)S(1)}, u32[]{:S(2)}) copy-start(f32[1024,640]{1,0:T(8,128)S(1)} %get-tuple-element.113) | copy-start | bytes 7864324
  191.8 30.4 %collective-permute-start.1 = (bf16[1,640,64]{1,2,0:T(8,128)(2,1)S(1)}, bf16[1,640,64]{1,2,0:T(8,128)(2,1)S(1)}, u32[]{:S(2)}, u32[]{:S(2)}) collective-permute-start(bf16[1,640,64]{1,2,0:T(8,128)(2,1)S(1)} %get-tuple-element.100), channel_id=1, source_target_pairs={{0,4},{1,5},{2,6},{3,7},{8,12},{9,13},{10,14},{11,15},{16,20},{17,... | collective-permute-start | bytes 245768 | tf_op jit(solution)/shard_map/ppermute | solution.py:61
  213.1 21.5 %collective-permute-start.3 = (bf16[1,640,64]{1,2,0:T(8,128)(2,1)S(1)}, bf16[1,640,64]{1,2,0:T(8,128)(2,1)S(1)}, u32[]{:S(2)}, u32[]{:S(2)}) collective-permute-start(bf16[1,640,64]{1,2,0:T(8,128)(2,1)S(1)} %get-tuple-element.99), channel_id=1, source_target_pairs={{4,0},{5,1},{6,2},{7,3},{12,8},{13,9},{14,10},{15,11},{20,16},{21,... | collective-permute-start | bytes 245768 | tf_op jit(solution)/shard_map/ppermute | solution.py:62
  222.2 2.9 copy-start.5
  256.2 12.4 %copy-start.9 = (f32[1024,640]{1,0:T(8,128)}, f32[1024,640]{1,0:T(8,128)S(1)}, u32[]{:S(2)}) copy-start(f32[1024,640]{1,0:T(8,128)S(1)} %get-tuple-element.115) | copy-start | bytes 7864324
  256.7 11.8 %copy-start.13 = (bf16[640,1280]{1,0:T(8,128)(2,1)S(1)}, bf16[640,1280]{1,0:T(8,128)(2,1)}, u32[]{:S(2)}) copy-start(bf16[640,1280]{1,0:T(8,128)(2,1)} %reshape.1490) | copy-start | bytes 4915204
  289.5 34.6 %collective-permute-start.8 = (bf16[1,640,64]{1,2,0:T(8,128)(2,1)S(1)}, bf16[1,640,64]{1,2,0:T(8,128)(2,1)S(1)}, u32[]{:S(2)}, u32[]{:S(2)}) collective-permute-start(bf16[1,640,64]{1,2,0:T(8,128)(2,1)S(1)} %get-tuple-element.97), channel_id=1, source_target_pairs={{0,4},{1,5},{2,6},{3,7},{8,12},{9,13},{10,14},{11,15},{16,20},{17,... | collective-permute-start | bytes 245768 | tf_op jit(solution)/shard_map/ppermute | solution.py:61
  292.6 30.6 %collective-permute-start.7 = (bf16[1,640,64]{1,2,0:T(8,128)(2,1)S(1)}, bf16[1,640,64]{1,2,0:T(8,128)(2,1)S(1)}, u32[]{:S(2)}, u32[]{:S(2)}) collective-permute-start(bf16[1,640,64]{1,2,0:T(8,128)(2,1)S(1)} %get-tuple-element.98), channel_id=1, source_target_pairs={{4,0},{5,1},{6,2},{7,3},{12,8},{13,9},{14,10},{15,11},{20,16},{21,... | collective-permute-start | bytes 245768 | tf_op jit(solution)/shard_map/ppermute | solution.py:62
  326.9 13.6 %copy-start.3 = (f32[1024,640]{1,0:T(8,128)S(1)}, f32[1024,640]{1,0:T(8,128)}, u32[]{:S(2)}) copy-start(f32[1024,640]{1,0:T(8,128)} %copy-done.1) | copy-start | bytes 7864324
  349.9 3.5 copy-start.15
  349.9 3.5 copy-start.17
  349.9 3.5 copy-start.19
  349.9 3.5 copy-start.21
  381.6 47.6 %copy-start.8 = (f32[4,204800]{1,0:T(4,128)S(1)}, f32[4,204800]{1,0:T(4,128)}, u32[]{:S(2)}) copy-start(f32[4,204800]{1,0:T(4,128)} %reshape.1509) | copy-start | bytes 9830404
  429.2 17.3 %copy-start.23 = (f32[4,320]{1,0:T(4,128)S(1)}, f32[4,320]{1,0:T(4,128)}, u32[]{:S(2)}) copy-start(f32[4,320]{1,0:T(4,128)} %convert_reduce_fusion.3) | copy-start | bytes 15364
  472.0 157.5 %reduce-scatter.8.cloned.1.call-start = ((), (), s32[]{:S(2)}) async-start(), calls=%async_computation.7 | async-start | bytes 9256960 | tf_op jit(solution)/shard_map/reduce_scatter | solution.py:258
  497.0 170.2 %copy-start.22 = (f32[4,320]{1,0:T(4,128)S(1)}, f32[4,320]{1,0:T(4,128)}, u32[]{:S(2)}) copy-start(f32[4,320]{1,0:T(4,128)} %get-tuple-element.108) | copy-start | bytes 15364
  497.0 170.1 %reduce-scatter.10.cloned.1.call-start = ((), (), s32[]{:S(2)}) async-start(), calls=%async_computation.9 | async-start | bytes 2314240
  629.5 122.7 %all-gather.7.cloned.1.call-start = ((), (), s32[]{:S(2)}) async-start(), calls=%async_computation.8 | async-start | bytes 4165632 | tf_op jit(solution)/shard_map/all_gather | solution.py:260
  667.2 5.1 copy-start.10
  687.0 4.8 copy-start.7
  688.4 18.9 %collective-permute-start.6 = (bf16[1,320,1024]{2,1,0:T(8,128)(2,1)}, bf16[1,320,1024]{2,1,0:T(8,128)(2,1)}, u32[]{:S(2)}, u32[]{:S(2)}) collective-permute-start(bf16[1,320,1024]{2,1,0:T(8,128)(2,1)} %get-tuple-element.94), channel_id=1, source_target_pairs={{0,3},{1,2},{2,1},{3,0},{4,7},{5,6},{6,5},{7,4},{8,11},{9,10},{10,... | collective-permute-start | bytes 1966088 | tf_op jit(solution)/shard_map/ppermute | solution.py:91
  689.8 31.6 %collective-permute-start.5 = (bf16[1,320,1024]{2,1,0:T(8,128)(2,1)}, bf16[1,320,1024]{2,1,0:T(8,128)(2,1)}, u32[]{:S(2)}, u32[]{:S(2)}) collective-permute-start(bf16[1,320,1024]{2,1,0:T(8,128)(2,1)} %get-tuple-element.95), channel_id=1, source_target_pairs={{0,2},{1,3},{2,0},{3,1},{4,6},{5,7},{6,4},{7,5},{8,10},{9,11},{10,... | collective-permute-start | bytes 1966088 | tf_op jit(solution)/shard_map/ppermute | solution.py:91
  691.2 30.2 %collective-permute-start.4 = (bf16[1,320,1024]{2,1,0:T(8,128)(2,1)}, bf16[1,320,1024]{2,1,0:T(8,128)(2,1)}, u32[]{:S(2)}, u32[]{:S(2)}) collective-permute-start(bf16[1,320,1024]{2,1,0:T(8,128)(2,1)} %get-tuple-element.96), channel_id=1, source_target_pairs={{0,1},{1,0},{2,3},{3,2},{4,5},{5,4},{6,7},{7,6},{8,9},{9,8},{10,11... | collective-permute-start | bytes 1966088 | tf_op jit(solution)/shard_map/ppermute | solution.py:91
  702.8 32.6 %collective-permute-start.11 = (bf16[1,320,1024]{2,1,0:T(8,128)(2,1)}, bf16[1,320,1024]{2,1,0:T(8,128)(2,1)}, u32[]{:S(2)}, u32[]{:S(2)}) collective-permute-start(bf16[1,320,1024]{2,1,0:T(8,128)(2,1)} %get-tuple-element.90), channel_id=1, source_target_pairs={{0,3},{1,2},{2,1},{3,0},{4,7},{5,6},{6,5},{7,4},{8,11},{9,10},{10,... | collective-permute-start | bytes 1966088 | tf_op jit(solution)/shard_map/ppermute | solution.py:91
  704.2 43.9 %collective-permute-start.10 = (bf16[1,320,1024]{2,1,0:T(8,128)(2,1)}, bf16[1,320,1024]{2,1,0:T(8,128)(2,1)}, u32[]{:S(2)}, u32[]{:S(2)}) collective-permute-start(bf16[1,320,1024]{2,1,0:T(8,128)(2,1)} %get-tuple-element.91), channel_id=1, source_target_pairs={{0,2},{1,3},{2,0},{3,1},{4,6},{5,7},{6,4},{7,5},{8,10},{9,11},{10,... | collective-permute-start | bytes 1966088 | tf_op jit(solution)/shard_map/ppermute | solution.py:91
  707.2 41.0 %collective-permute-start.9 = (bf16[1,320,1024]{2,1,0:T(8,128)(2,1)}, bf16[1,320,1024]{2,1,0:T(8,128)(2,1)}, u32[]{:S(2)}, u32[]{:S(2)}) collective-permute-start(bf16[1,320,1024]{2,1,0:T(8,128)(2,1)} %get-tuple-element.92), channel_id=1, source_target_pairs={{0,1},{1,0},{2,3},{3,2},{4,5},{5,4},{6,7},{7,6},{8,9},{9,8},{10,11... | collective-permute-start | bytes 1966088 | tf_op jit(solution)/shard_map/ppermute | solution.py:91
  723.2 25.1 %copy-start.12 = (bf16[1,1,320,1024]{3,2,0,1:T(8,128)(2,1)S(1)}, bf16[1,1,320,1024]{3,2,0,1:T(8,128)(2,1)}, u32[]{:S(2)}) copy-start(bf16[1,1,320,1024]{3,2,0,1:T(8,128)(2,1)} %get-tuple-element.89) | copy-start | bytes 1966084
  (4 other events, 8.3 us)
Sparse Core Ops, SparseCore 0:
  13.4 131.5 all-gather.4
  472.1 24.7 reduce-scatter.5
  499.4 130.0 reduce-scatter.7
  632.4 34.6 reduce-scatter.9
  668.5 42.8 all-gather.6
